TPU v7x, 32 devices: a whole 2x2x4 slice. The times are simulated.
32 devices in a mesh: sta: 4 (over y, x), evt: 8 (over z, core).
Axes of the slice: x: 2, y: 2, z: 4, core: 2. Of those that a mesh axis runs over, the one named last changes fastest.
Arguments:
- traces: bfloat16 [3, 32, 512, 2048], P(None, 'sta', 'evt'), may hold values from -96 to 96
- baz_bin: int32 [32, 512], P('sta', 'evt'), may hold values from 0 to 35
- inc_bin: int32 [32, 512], P('sta', 'evt'), may hold values from 0 to 7
- counts: int32 [32], P('sta'), may hold values from 64 to 512
- depth_index: int32 [32, 512], P('sta'), may hold values from 0 to 2046
- tile_of: int32 [32], replicated, may hold values from 0 to 15
Outputs:
- stack: float32 [16, 5, 2, 512], P('sta', None, None, 'evt')
All inputs are finite; a program needn't handle non-finite values.
Results may differ from a plain program's by a relative error of at most 0.0003.
Values sent between devices are 32-bit elements; how exact they have to be, the bound alone decides.
A program may use at most 64 MiB of HBM per device.

v0:
```python
import jax
import jax.numpy as jnp
from jax import lax
from jax.sharding import PartitionSpec as P

NS = 2048
DEPTHS = 512
BAZ_BINS = 36
TILE_DEV = 4


def solve_blocks(normal, right):
    factor = jnp.linalg.cholesky(normal)
    middle = jax.scipy.linalg.solve_triangular(factor, right, lower=True)
    return jax.scipy.linalg.solve_triangular(factor, middle, lower=True, trans=1)


def to_depths(values, indices):
    picks = indices[:, None, None, :]
    first = jnp.take_along_axis(values, picks, axis=3)
    second = jnp.take_along_axis(values, picks + 1, axis=3)
    return 0.5 * (first + second)


def body(traces, baz_bin, inc_bin, counts, depth_index, tile_of):
    highest = lax.Precision.HIGHEST
    stations = traces.shape[1]
    slots = traces.shape[2]
    evt_count = lax.axis_size("evt")
    depth_share = DEPTHS // evt_count
    phi = (baz_bin.astype(jnp.float32) + 0.5) * (2.0 * jnp.pi / BAZ_BINS)
    incidence = (12.0 + 2.5 * (inc_bin.astype(jnp.float32) + 0.5)) * (jnp.pi / 180.0)
    cosine = jnp.cos(phi)[:, :, None]
    sine = jnp.sin(phi)[:, :, None]
    vertical = traces[0].astype(jnp.float32)
    north = traces[1].astype(jnp.float32)
    east = traces[2].astype(jnp.float32)
    radial = -(cosine * north + sine * east)
    quality = jnp.cos(incidence)[:, :, None] * radial + jnp.sin(incidence)[:, :, None] * vertical
    transverse = sine * north - cosine * east
    data = jnp.concatenate([quality, transverse], axis=2)
    slot_ids = lax.axis_index("evt") * slots + jnp.arange(slots)
    live = (slot_ids[None, :] < counts[:, None]).astype(jnp.float32)
    harm = jnp.stack(
        [jnp.ones_like(phi), jnp.cos(phi), jnp.sin(phi), jnp.cos(2.0 * phi), jnp.sin(2.0 * phi)],
        axis=2,
    )
    weighted = harm * live[:, :, None]
    normal_part = jnp.einsum("sek,sel->skl", weighted, harm, precision=highest)
    rhs_part = jnp.einsum("sek,sec->skc", weighted, data, precision=highest)
    normal = lax.psum(normal_part, "evt") + jnp.eye(5, dtype=jnp.float32)[None]
    shares = lax.psum_scatter(rhs_part, "evt", scatter_dimension=2, tiled=True)
    solved = solve_blocks(normal, shares)
    coeff = lax.all_gather(solved, "evt", axis=2, tiled=True).reshape(stations, 5, 2, NS)
    mine = lax.dynamic_slice_in_dim(
        depth_index, lax.axis_index("evt") * depth_share, depth_share, 1
    )
    profile = to_depths(coeff, mine)
    first_tile = lax.axis_index("sta") * TILE_DEV
    own_tiles = first_tile + jnp.arange(TILE_DEV)
    members = jnp.sum((tile_of[None, :] == own_tiles[:, None]).astype(jnp.float32), axis=1)
    everyone = lax.all_gather(profile, "sta", axis=0, tiled=True)
    onehot = (tile_of[None, :] == own_tiles[:, None]).astype(jnp.float32)
    sums = jnp.einsum("ts,skcz->tkcz", onehot, everyone, precision=highest)
    return sums / jnp.maximum(members, 1.0)[:, None, None, None]


def solution(mesh):
    return jax.shard_map(
        body,
        mesh=mesh,
        in_specs=(
            P(None, "sta", "evt", None),
            P("sta", "evt"),
            P("sta", "evt"),
            P("sta"),
            P("sta", None),
            P(),
        ),
        out_specs=P("sta", None, None, "evt"),
        check_vma=False,
    )
```

profile of v0, /device:TPU:0, one launch (start us, length us, event | category | flops | bytes accessed | tf_op | source)
XLA Modules:
  0.0 130.2 jit_solution(14801742810654873437)
XLA Ops:
  6.5 0.8 fusion.24
  7.3 0.7 compare_convert_fusion
  8.0 6.8 %fusion.7 = (f32[8,64,2048]{2,1,0:T(8,128)}, f32[8,64,2048]{2,1,0:T(8,128)}) fusion(bf16[3,8,64,2048]{3,2,1,0:T(8,128)(2,1)} %param.8, f32[8,64]{1,0:T(8,128)S(1)} %get-tuple-element.18, f32[8,64]{1,0:T(8,128)S(1)} %get-tuple-element.13, f32[8,64]{1,0:T(8,128)S(1)} %get-tuple-element.15, f32[8,64]{1,0:T(8,128)S(1)} %get-tuple-element.19), kind=kLoop, calls=%fused_computation.13 | loop fusion | flops 13631488 | bytes 14688256 | tf_op jit(solution)/shard_map/add | solution.py:39
  14.9 0.0 copy-start.1
  14.9 7.3 %fusion = f32[8,5,4096]{2,1,0:T(8,128)} fusion(f32[8,64,2048]{2,1,0:T(8,128)} %get-tuple-element.7, f32[8,64,2048]{2,1,0:T(8,128)} %get-tuple-element.6, f32[8,64,5]{1,2,0:T(8,128)S(1)} %stack.19, f32[8,64]{1,0:T(8,128)S(1)} %compare_convert_fusion), kind=kOutput, calls=%fused_computation.2 | convolution fusion | flops 127928832 | bytes 9056256 | tf_op jit(solution)/shard_map/sek,sec->skc/dot_general | solution.py:50
  22.2 0.0 reduce-scatter.2.cloned.1.call-update
  22.2 0.2 fusion.10
  22.4 30.3 %psum.7 = f32[8,5,5]{1,2,0:T(8,128)S(1)} all-reduce(f32[8,5,5]{1,2,0:T(8,128)S(1)} %fusion.10), channel_id=1, replica_groups=mesh['sta'=4,'evt'=8] {'evt'}, use_global_device_ids=true, to_apply=%region_0.0 | all-reduce | flops 200 | bytes 1600 | tf_op jit(solution)/shard_map/psum | solution.py:51
  52.8 0.1 copy.30
  52.9 0.1 copy.31
  53.0 3.7 %custom-call.11 = f32[8,5,5]{2,1,0:T(8,128)S(1)} custom-call(f32[8,5,5]{2,1,0:T(8,128)S(1)} %fusion.17), custom_call_target="Cholesky" | custom-call | tf_op jit(solution)/shard_map/jit(cholesky)/cholesky | solution.py:13
  56.7 0.1 compare_reduce_fusion
  56.9 0.1 select_bitcast_fusion
  56.9 3.2 %custom-call.12 = f32[8,1,5,5]{2,3,1,0:T(8,128)S(1)} custom-call(f32[8,1,5,5]{3,2,1,0:T(8,128)S(1)} %select_bitcast_fusion), custom_call_target="InvertDiagBlocksLowerTriangular" | custom-call | tf_op jit(solution)/shard_map/jit(_solve_triangular)/vmap()/triangular_solve | solution.py:15
  60.1 0.1 bitcast_or_fusion.1
  60.2 0.1 reshape.123
  60.3 0.1 reshape.128
  60.4 0.1 and_bitcast_fusion.1
  60.5 0.2 fusion.28
  60.7 0.0 reduce-scatter.2.cloned.1.call-done
  60.7 1.2 fusion.15
  61.9 0.3 fusion.13
  62.2 16.4 %all_gather.6 = f32[8,5,4096]{2,1,0:T(8,128)S(1)} all-gather(f32[8,5,512]{2,1,0:T(8,128)S(1)} %fusion.13), channel_id=1, replica_groups=mesh['sta'=4,'evt'=8] {'evt'}, dimensions={2}, use_global_device_ids=true | all-gather | bytes 737280 | tf_op jit(solution)/shard_map/all_gather | solution.py:54
  78.5 0.6 reshape.133
  79.1 17.0 %copy.34 = f32[8,5,2,2048]{1,2,3,0:T(2,128)} copy(f32[8,5,2,2048]{3,2,1,0:T(2,128)S(1)} %reshape.133) | data formatting | bytes 1310720 | tf_op jit(solution)/shard_map/reshape | solution.py:54
  96.1 8.3 %gather_fusion = f32[512,5,2]{1,2,0:T(2,128)S(1)} fusion(f32[8,5,2,2048]{1,2,3,0:T(2,128)} %copy.34, s32[512]{0:T(512)S(1)} %reshape.123), kind=kCustom, calls=%fused_computation.clone | custom fusion | bytes 45056 | tf_op jit(solution)/shard_map/jit(take_along_axis)/gather | solution.py:20
  104.4 0.2 copy.44
  104.6 8.3 %gather_fusion.1 = f32[512,5,2]{1,2,0:T(2,128)S(1)} fusion(f32[8,5,2,2048]{1,2,3,0:T(2,128)} %copy.34, s32[512]{0:T(512)S(1)} %reshape.128), kind=kCustom, calls=%fused_computation.1.clone | custom fusion | bytes 45056 | tf_op jit(solution)/shard_map/jit(take_along_axis)/gather | solution.py:21
  113.0 0.2 copy.46
  113.2 9.3 %all_gather.7 = f32[32,5,2,64]{3,0,2,1:T(8,128)S(1)} all-gather(f32[8,5,2,64]{3,0,2,1:T(8,128)S(1)} %fusion.12), channel_id=1, replica_groups=mesh['sta'=4,'evt'=8] {'sta'}, dimensions={0}, use_global_device_ids=true | all-gather | bytes 102400 | tf_op jit(solution)/shard_map/all_gather | solution.py:62
  122.6 0.2 convolution_divide_fusion
  122.8 0.6 copy.38
  (16 shorter events, 0.1 us)
Async XLA Ops:
  6.5 54.2 %reduce-scatter.2.cloned.1.call-start = ((), (), s32[]{:S(2)}) async-start(), calls=%async_computation.1 | async-start | bytes 1179648 | tf_op jit(solution)/shard_map/reduce_scatter | solution.py:52
  14.9 45.2 %copy-start = (s32[8,512]{1,0:T(8,128)S(1)}, s32[8,512]{1,0:T(8,128)}, u32[]{:S(2)}) copy-start(s32[8,512]{1,0:T(8,128)} %param.12) | copy-start | bytes 49156
  14.9 45.6 %copy-start.1 = (s32[32]{0:T(128)S(1)}, s32[32]{0:T(128)}, u32[]{:S(2)}) copy-start(s32[32]{0:T(128)} %param.13) | copy-start | bytes 388
Sparse Core Ops, SparseCore 0:
  22.3 35.4 reduce-scatter.1
where the time goes:
time: 131 us; the launch traced here: 130 us
  blocking collectives  56 us (43%)
  local copies, waits for them, and re-layouts  35.7 us (27%)
  other arithmetic  15.8 us (12%)
  between operations  13.5 us (10%)
  matrix products  9.13 us (7%)
    psum x1, blocking collectives, body(): normal = lax.psum(normal_part, 'evt') + jnp.eye(5, dtype=jnp.float32)[None]  30.3 us
    reshape x2, local copies, waits for them, and re-layouts, body(): lax.all_gather(solved, 'evt', axis=2, tiled=True)  17.5 us
    all_gather x1, blocking collectives, body(): lax.all_gather(solved, 'evt', axis=2, tiled=True)  16.4 us
    all_gather x1, blocking collectives, body(): everyone = lax.all_gather(profile, 'sta', axis=0, tiled=True)  9.34 us
    gather x3, local copies, waits for them, and re-layouts, to_depths(): second = jnp.take_along_axis(values, picks + 1, axis=3)  8.62 us
    gather x3, local copies, waits for them, and re-layouts, to_depths(): first = jnp.take_along_axis(values, picks, axis=3)  8.62 us
    dot_general x1, matrix products, body(): rhs_part = jnp.einsum('sek,sec->skc', weighted, data, precision=highest)  7.27 us
    add x1, other arithmetic, body(): jnp.cos(incidence)[:, :, None] * radial  6.81 us
  transfers between devices with their start and end apart: 1, of which 0 were waited for; matrix products, arithmetic and copies ran while one was open for 6% of the time, Pallas kernels for 0%

commit v1 on v0

--- a/solution.py
+++ b/solution.py
@@ -7,6 +7,22 @@
 DEPTHS = 512
 BAZ_BINS = 36
 TILE_DEV = 4
+
+
+def summed_both_ways(x, axis, dim, contribution):
+    count, position, rows = (lax.axis_size(axis), lax.axis_index(axis), x.shape[dim])
+    upward = [(i, (i + 1) % count) for i in range(count)]
+    backward = [(i, (i - 1) % count) for i in range(count)]
+    middle = count // 2
+    from_left = from_right = x
+    running = contribution(x, position * rows)
+    for step in range(1, middle + 1):
+        from_left = lax.ppermute(from_left, axis, upward)
+        if step < count - middle:
+            from_right = lax.ppermute(from_right, axis, backward)
+            running = running + contribution(from_right, (position + step) % count * rows)
+        running = running + contribution(from_left, (position - step) % count * rows)
+    return running
 
 
 def solve_blocks(normal, right):
@@ -59,9 +75,18 @@
     first_tile = lax.axis_index("sta") * TILE_DEV
     own_tiles = first_tile + jnp.arange(TILE_DEV)
     members = jnp.sum((tile_of[None, :] == own_tiles[:, None]).astype(jnp.float32), axis=1)
-    everyone = lax.all_gather(profile, "sta", axis=0, tiled=True)
     onehot = (tile_of[None, :] == own_tiles[:, None]).astype(jnp.float32)
-    sums = jnp.einsum("ts,skcz->tkcz", onehot, everyone, precision=highest)
+    sums = summed_both_ways(
+        profile,
+        "sta",
+        0,
+        lambda own_block, at: jnp.einsum(
+            "ts,skcz->tkcz",
+            lax.dynamic_slice_in_dim(onehot, at, own_block.shape[0], axis=1),
+            own_block,
+            precision=highest,
+        ),
+    )
     return sums / jnp.maximum(members, 1.0)[:, None, None, None]
 
 

time: 131 us -> 134 us (1.023)
  blocking collectives: 56 us -> 46.7 us
  waiting for transfers between devices: 0.04 us -> 9.19 us
  starting transfers between devices: 0.01 us -> 2.79 us
    all_gather x1 -> x0, blocking collectives: 9.34 us -> none  [body(): everyone = lax.all_gather(profile, 'sta', axis=0, tiled=True)]
    ppermute x0 -> x3, waiting for transfers between devices: none -> 9.15 us  [the longest x2 9.15 us: summed_both_ways(): from_left = lax.ppermute(from_left, axis, upward)]
    ppermute x0 -> x3, starting transfers between devices: none -> 2.78 us  [the longest x1 2.78 us: summed_both_ways(): from_right = lax.ppermute(from_right, axis, backward)]
  transfers between devices with their start and end apart: 1 -> 4, of which waited for: 0 -> 2; matrix products, arithmetic and copies ran while one was open for 6% -> 7% of each run, Pallas kernels for 0% -> 0%
where the time goes in v1:
time: 134 us
  blocking collectives  46.7 us (35%)
  local copies, waits for them, and re-layouts  35.7 us (27%)
  other arithmetic  15.8 us (12%)
  between operations  13.6 us (10%)
  matrix products  9.76 us (7%)
  waiting for transfers between devices  9.19 us (7%)
  starting transfers between devices  2.79 us (2%)
    psum x1, blocking collectives, body(): normal = lax.psum(normal_part, 'evt') + jnp.eye(5, dtype=jnp.float32)[None]  30.3 us
    reshape x2, local copies, waits for them, and re-layouts, body(): lax.all_gather(solved, 'evt', axis=2, tiled=True)  17.5 us
    all_gather x1, blocking collectives, body(): lax.all_gather(solved, 'evt', axis=2, tiled=True)  16.4 us
    ppermute x2, waiting for transfers between devices, summed_both_ways(): from_left = lax.ppermute(from_left, axis, upward)  9.15 us
    gather x3, local copies, waits for them, and re-layouts, to_depths(): second = jnp.take_along_axis(values, picks + 1, axis=3)  8.62 us
    gather x3, local copies, waits for them, and re-layouts, to_depths(): first = jnp.take_along_axis(values, picks, axis=3)  8.62 us
    dot_general x1, matrix products, body(): rhs_part = jnp.einsum('sek,sec->skc', weighted, data, precision=highest)  7.27 us
    add x1, other arithmetic, body(): jnp.cos(incidence)[:, :, None] * radial  6.81 us
  transfers between devices with their start and end apart: 4, of which 2 were waited for; matrix products, arithmetic and copies ran while one was open for 7% of the time, Pallas kernels for 0%

profile of v1, /device:TPU:0, one launch (start us, length us, event | category | flops | bytes accessed | tf_op | source)
XLA Modules:
  0.0 133.5 jit_solution(9072047489347087978)
XLA Ops:
  6.5 0.8 fusion.25
  7.3 0.7 compare_convert_fusion
  8.0 6.8 %fusion.7 = (f32[8,64,2048]{2,1,0:T(8,128)}, f32[8,64,2048]{2,1,0:T(8,128)}) fusion(bf16[3,8,64,2048]{3,2,1,0:T(8,128)(2,1)} %param.8, f32[8,64]{1,0:T(8,128)S(1)} %get-tuple-element.20, f32[8,64]{1,0:T(8,128)S(1)} %get-tuple-element.15, f32[8,64]{1,0:T(8,128)S(1)} %get-tuple-element.17, f32[8,64]{1,0:T(8,128)S(1)} %get-tuple-element.21), kind=kLoop, calls=%fused_computation.13 | loop fusion | flops 13631488 | bytes 14688256 | tf_op jit(solution)/shard_map/add | solution.py:55
  14.9 7.3 %fusion = f32[8,5,4096]{2,1,0:T(8,128)} fusion(f32[8,64,2048]{2,1,0:T(8,128)} %get-tuple-element.9, f32[8,64,2048]{2,1,0:T(8,128)} %get-tuple-element.8, f32[8,64,5]{1,2,0:T(8,128)S(1)} %stack.19, f32[8,64]{1,0:T(8,128)S(1)} %compare_convert_fusion), kind=kOutput, calls=%fused_computation.2 | convolution fusion | flops 127928832 | bytes 9056256 | tf_op jit(solution)/shard_map/sek,sec->skc/dot_general | solution.py:66
  22.2 0.2 fusion.11
  22.5 30.3 %psum.7 = f32[8,5,5]{1,2,0:T(8,128)S(1)} all-reduce(f32[8,5,5]{1,2,0:T(8,128)S(1)} %fusion.11), channel_id=1, replica_groups=mesh['sta'=4,'evt'=8] {'evt'}, use_global_device_ids=true, to_apply=%region_0.0 | all-reduce | flops 200 | bytes 1600 | tf_op jit(solution)/shard_map/psum | solution.py:67
  52.8 0.1 copy.30
  52.9 0.1 copy.31
  53.1 3.7 %custom-call.11 = f32[8,5,5]{2,1,0:T(8,128)S(1)} custom-call(f32[8,5,5]{2,1,0:T(8,128)S(1)} %fusion.18), custom_call_target="Cholesky" | custom-call | tf_op jit(solution)/shard_map/jit(cholesky)/cholesky | solution.py:29
  56.8 0.1 compare_reduce_fusion
  56.9 0.1 select_bitcast_fusion
  57.0 3.2 %custom-call.12 = f32[8,1,5,5]{2,3,1,0:T(8,128)S(1)} custom-call(f32[8,1,5,5]{3,2,1,0:T(8,128)S(1)} %select_bitcast_fusion), custom_call_target="InvertDiagBlocksLowerTriangular" | custom-call | tf_op jit(solution)/shard_map/jit(_solve_triangular)/vmap()/triangular_solve | solution.py:31
  60.2 0.1 bitcast_or_fusion.1
  60.4 0.1 and_bitcast_fusion.1
  60.5 0.2 convert_reduce_fusion
  60.8 1.2 fusion.16
  62.0 0.3 fusion.14
  62.2 16.4 %all_gather.3 = f32[8,5,4096]{2,1,0:T(8,128)S(1)} all-gather(f32[8,5,512]{2,1,0:T(8,128)S(1)} %fusion.14), channel_id=1, replica_groups=mesh['sta'=4,'evt'=8] {'evt'}, dimensions={2}, use_global_device_ids=true | all-gather | bytes 737280 | tf_op jit(solution)/shard_map/all_gather | solution.py:70
  78.6 0.6 reshape.136
  79.2 17.0 %copy.34 = f32[8,5,2,2048]{1,2,3,0:T(2,128)} copy(f32[8,5,2,2048]{3,2,1,0:T(2,128)S(1)} %reshape.136) | data formatting | bytes 1310720 | tf_op jit(solution)/shard_map/reshape | solution.py:70
  96.1 8.3 %gather_fusion = f32[512,5,2]{1,2,0:T(2,128)S(1)} fusion(f32[8,5,2,2048]{1,2,3,0:T(2,128)} %copy.34, s32[512]{0:T(512)S(1)} %reshape.123), kind=kCustom, calls=%fused_computation.clone | custom fusion | bytes 45056 | tf_op jit(solution)/shard_map/jit(take_along_axis)/gather | solution.py:36
  104.5 0.2 copy.47
  104.7 8.3 %gather_fusion.1 = f32[512,5,2]{1,2,0:T(2,128)S(1)} fusion(f32[8,5,2,2048]{1,2,3,0:T(2,128)} %copy.34, s32[512]{0:T(512)S(1)} %reshape.128), kind=kCustom, calls=%fused_computation.1.clone | custom fusion | bytes 45056 | tf_op jit(solution)/shard_map/jit(take_along_axis)/gather | solution.py:37
  113.0 0.2 copy.49
  113.3 2.8 %collective-permute-start = (f32[8,5,2,64]{3,0,2,1:T(8,128)S(1)}, f32[8,5,2,64]{3,0,2,1:T(8,128)S(1)}, u32[]{:S(2)}, u32[]{:S(2)}) collective-permute-start(f32[8,5,2,64]{3,0,2,1:T(8,128)S(1)} %fusion.13), channel_id=1, source_target_pairs={{0,24},{8,0},{16,8},{24,16},{1,25},{9,1},{17,9},{25,17},{2,26},{10... | collective-permute-start | bytes 61448 | tf_op jit(solution)/shard_map/ppermute | solution.py:22
  116.0 0.2 fusion.32
  116.3 4.7 %collective-permute-done.1 = f32[8,5,2,64]{3,0,2,1:T(8,128)S(1)} collective-permute-done((f32[8,5,2,64]{3,0,2,1:T(8,128)S(1)}, f32[8,5,2,64]{3,0,2,1:T(8,128)S(1)}, u32[]{:S(2)}, u32[]{:S(2)}) %collective-permute-start.1) | collective-permute-done | bytes 20512 | tf_op jit(solution)/shard_map/ppermute | solution.py:20
  121.0 0.2 convolution_add_fusion.2
  121.2 0.2 convolution_add_fusion.1
  121.4 4.5 %collective-permute-done.2 = f32[8,5,2,64]{3,0,2,1:T(8,128)S(1)} collective-permute-done((f32[8,5,2,64]{3,0,2,1:T(8,128)S(1)}, f32[8,5,2,64]{3,0,2,1:T(8,128)S(1)}, u32[]{:S(2)}, u32[]{:S(2)}) %collective-permute-start.2) | collective-permute-done | bytes 20512 | tf_op jit(solution)/shard_map/ppermute | solution.py:20
  125.8 0.2 fusion.9
  126.1 0.6 copy.38
  (24 shorter events, 0.3 us)
Async XLA Ops:
  6.5 54.2 %reduce-scatter.2.cloned.1.call-start = ((), (), s32[]{:S(2)}) async-start(), calls=%async_computation.1 | async-start | bytes 1179648 | tf_op jit(solution)/shard_map/reduce_scatter | solution.py:68
  14.9 45.3 %copy-start = (s32[8,512]{1,0:T(8,128)S(1)}, s32[8,512]{1,0:T(8,128)}, u32[]{:S(2)}) copy-start(s32[8,512]{1,0:T(8,128)} %param.12) | copy-start | bytes 49156
  14.9 45.6 %copy-start.1 = (s32[32]{0:T(128)S(1)}, s32[32]{0:T(128)}, u32[]{:S(2)}) copy-start(s32[32]{0:T(128)} %param.13) | copy-start | bytes 388
  113.3 7.7 %collective-permute-start = (f32[8,5,2,64]{3,0,2,1:T(8,128)S(1)}, f32[8,5,2,64]{3,0,2,1:T(8,128)S(1)}, u32[]{:S(2)}, u32[]{:S(2)}) collective-permute-start(f32[8,5,2,64]{3,0,2,1:T(8,128)S(1)} %fusion.13), channel_id=1, source_target_pairs={{0,24},{8,0},{16,8},{24,16},{1,25},{9,1},{17,9},{25,17},{2,26},{10... | collective-permute-start | bytes 61448 | tf_op jit(solution)/shard_map/ppermute | solution.py:22
  116.0 4.9 %collective-permute-start.1 = (f32[8,5,2,64]{3,0,2,1:T(8,128)S(1)}, f32[8,5,2,64]{3,0,2,1:T(8,128)S(1)}, u32[]{:S(2)}, u32[]{:S(2)}) collective-permute-start(f32[8,5,2,64]{3,0,2,1:T(8,128)S(1)} %fusion.13), channel_id=1, source_target_pairs={{0,8},{8,16},{16,24},{24,0},{1,9},{9,17},{17,25},{25,1},{2,10},{10... | collective-permute-start | bytes 61448 | tf_op jit(solution)/shard_map/ppermute | solution.py:20
  120.9 4.9 %collective-permute-start.2 = (f32[8,5,2,64]{3,0,2,1:T(8,128)S(1)}, f32[8,5,2,64]{3,0,2,1:T(8,128)S(1)}, u32[]{:S(2)}, u32[]{:S(2)}) collective-permute-start(f32[8,5,2,64]{3,0,2,1:T(8,128)S(1)} %collective-permute-done.1), channel_id=1, source_target_pairs={{0,8},{8,16},{16,24},{24,0},{1,9},{9,17},{17,25},{25,1},{2,10},{10... | collective-permute-start | bytes 61448 | tf_op jit(solution)/shard_map/ppermute | solution.py:20
Sparse Core Ops, SparseCore 0:
  22.3 35.4 reduce-scatter.1
